TPU v7x, 256 devices: a whole 4x4x8 slice. The times are simulated.
256 devices in a mesh: leaf: 8 (over z), trunk: 32 (over y, x, core).
Axes of the slice: x: 4, y: 4, z: 8, core: 2. Of those that a mesh axis runs over, the one named last changes fastest.
Arguments:
- trunk_tokens: bfloat16 [16, 8192, 1024], P('leaf', 'trunk'), may hold values from -6 to 6
- branch_tokens: bfloat16 [2048, 128, 1024], P(('leaf', 'trunk')), may hold values from -6 to 6
- fork_offset: int32 [8, 32, 8], P('leaf', 'trunk'), may hold values from 0 to 255
- fork_tree: int32 [8, 32, 8], P('leaf', 'trunk'), may hold values from 0 to 1
- branch_len: int32 [2048], P(('leaf', 'trunk')), may hold values from 0 to 128, as said below
- w_query: bfloat16 [1024, 1024], P('trunk'), may hold values from -0.1875 to 0.1875
- w_key: bfloat16 [1024, 1024], P('trunk'), may hold values from -0.1875 to 0.1875
- w_value: bfloat16 [1024, 1024], P('trunk'), may hold values from -0.1875 to 0.1875
- w_out: bfloat16 [1024, 1024], P('trunk'), may hold values from -0.1875 to 0.1875
Outputs:
- mixed: bfloat16 [2048, 128, 1024], P(('leaf', 'trunk'))
Inputs may be any that keep to these rules, and one draw needn't show every extreme that they name: `branch_len`: each length is a multiple of 128; some slot has the full 128 in every draw.
All inputs are finite; a program needn't handle non-finite values.
Results may differ from a plain program's by a relative error of at most 0.0065.
Values may be sent and summed in bfloat16 or wider, within the bound.
A program may use at most 128 MiB of HBM per device.

v0:
```python
import jax
import jax.numpy as jnp
from jax import lax
from jax.sharding import Mesh
from jax.sharding import PartitionSpec as P

H = 8
DH = 128
TRUNK = ("trunk_0", "trunk_1", "trunk_2")
LEAF_TRUNK = ("leaf", "trunk_0", "trunk_1", "trunk_2")


def side_by_side(arrays, axis, dim, along):
    ends, at = ([], 0)
    for a in arrays[:-1]:
        at += a.shape[along]
        ends.append(at)
    both = jnp.concatenate(arrays, axis=along)
    return tuple(jnp.split(lax.all_gather(both, axis, axis=dim, tiled=True), ends, axis=along))


def neutral_like(value, identity):
    return jnp.broadcast_to(jnp.asarray(identity, value.dtype), value.shape)


def entering(value, axes, combine, identity):
    before = start = neutral_like(value, identity)
    subtotal = value
    for axis in reversed(axes):
        peers, place = (lax.axis_size(axis), lax.axis_index(axis))
        pieces = lax.all_gather(subtotal, axis)
        inside, subtotal = (start, start)
        for k in range(peers):
            passed = k < place
            subtotal = combine(subtotal, pieces[k])
            inside = jnp.where(passed, subtotal, inside)
        before = combine(inside, before)
    return before


def joined_along(parts, dim):
    parts = jnp.moveaxis(parts, 0, dim)
    lengths = parts.shape
    return parts.reshape(*lengths[:dim], lengths[dim] * lengths[dim + 1], *lengths[dim + 2 :])


def all_blocks(value, axes, order):
    parts = value
    for k in order:
        parts = lax.all_gather(parts, axes[k])
    done = order[::-1]
    back = [done.index(k) for k in range(len(axes))]
    parts = parts.transpose(*back, *range(len(axes), parts.ndim))
    return parts.reshape(-1, *value.shape)


def whole_of(value, axes, order, dim):
    return joined_along(all_blocks(value, axes, order), dim)


def matmul(left, right):
    return jnp.dot(left, right, preferred_element_type=jnp.float32)


def add_states(earlier, later):
    return earlier + later


def shards(
    trunk_tokens, branch_tokens, fork_offset, fork_tree, branch_len, w_query, w_key, w_value, w_out
):
    trees, trunk_tok, width = trunk_tokens.shape
    slots, blen, _ = branch_tokens.shape
    heads_dim = w_key.shape[1]
    trunk_rows = trunk_tokens.reshape(trees * trunk_tok, width)
    branch_rows = branch_tokens.reshape(slots * blen, width)
    full_query, full_key, full_value = side_by_side((w_query, w_key, w_value), TRUNK, 0, 1)
    trunk_key = matmul(trunk_rows, full_key)
    trunk_value = matmul(trunk_rows, full_value)
    branch_query = matmul(branch_rows, full_query)
    branch_key = matmul(branch_rows, full_key)
    branch_value = matmul(branch_rows, full_value)
    trunk_key = trunk_key.astype(jnp.bfloat16)
    trunk_value = trunk_value.astype(jnp.bfloat16)
    key_four = trunk_key.reshape(trees, trunk_tok, H, DH)
    value_four = trunk_value.reshape(trees, trunk_tok, H, DH)
    totals = jnp.einsum("rthd,rthf->rhdf", key_four, value_four, preferred_element_type=jnp.float32)
    carried = entering(totals, TRUNK, add_states, jnp.zeros_like(totals))
    entries = fork_offset.shape[2]
    offsets = fork_offset.reshape(entries)
    which_tree = fork_tree.reshape(entries)
    positions = jnp.arange(trees * trunk_tok, dtype=jnp.int32)
    tree_of = positions // trunk_tok
    place_in = positions % trunk_tok
    selected_rows = (tree_of[None, :] == which_tree[:, None]) & (
        place_in[None, :] < offsets[:, None]
    )
    masked_key = selected_rows.astype(jnp.bfloat16)[:, :, None] * trunk_key[None]
    masked_key = masked_key.reshape(entries, trees * trunk_tok, H, DH)
    partial_value = jnp.einsum(
        "erhd,rhf->ehdf",
        masked_key,
        trunk_value.reshape(trees * trunk_tok, H, DH),
        preferred_element_type=jnp.float32,
    )
    tree_pick = (jnp.arange(trees, dtype=jnp.int32)[None, :] == which_tree[:, None]).astype(
        jnp.float32
    )
    chosen = jnp.sum(tree_pick[:, :, None, None, None] * carried[None], axis=1)
    fork_state = chosen + partial_value
    query = branch_query.astype(jnp.bfloat16).reshape(slots, blen, H, DH)
    key = branch_key.astype(jnp.bfloat16).reshape(slots, blen, H, DH)
    value = branch_value.astype(jnp.bfloat16).reshape(slots, blen, H, DH)
    arrived = lax.all_to_all(query, "leaf", split_axis=0, concat_axis=0, tiled=True)
    held_inter = jnp.einsum(
        "ebhd,ehdf->ebhf", arrived.astype(jnp.float32), fork_state, precision=lax.Precision.HIGHEST
    )
    inter = lax.all_to_all(held_inter, "leaf", split_axis=0, concat_axis=0, tiled=True)
    scores = jnp.einsum("sbhd,schd->shbc", query, key, preferred_element_type=jnp.float32)
    rows = jnp.arange(blen, dtype=jnp.int32)
    causal = rows[None, :] <= rows[:, None]
    weights = jnp.where(causal[None, None], scores, 0.0).astype(jnp.bfloat16)
    numerator = inter + jnp.einsum(
        "shbc,schf->sbhf", weights, value, preferred_element_type=jnp.float32
    )
    meansq = jnp.mean(numerator * numerator, axis=-1, keepdims=True)
    normed = (
        (numerator * lax.rsqrt(meansq + 1e-06))
        .astype(jnp.bfloat16)
        .reshape(slots * blen, heads_dim)
    )
    projected = matmul(normed, whole_of(w_out, TRUNK, (1, 0, 2), 0))
    live = rows[None, :] < branch_len[:, None]
    projected = projected.reshape(slots, blen, width)
    return jnp.where(live[:, :, None], projected, 0.0).astype(jnp.bfloat16)


def solution(mesh):
    split = Mesh(
        mesh.devices.reshape(mesh.shape["leaf"], 4, 4, 2), ("leaf", "trunk_0", "trunk_1", "trunk_2")
    )
    return jax.shard_map(
        shards,
        mesh=split,
        in_specs=(
            P("leaf", TRUNK, None),
            P(LEAF_TRUNK, None, None),
            P("leaf", TRUNK, None),
            P("leaf", TRUNK, None),
            P(LEAF_TRUNK),
            P(TRUNK, None),
            P(TRUNK, None),
            P(TRUNK, None),
            P(TRUNK, None),
        ),
        out_specs=P(LEAF_TRUNK, None, None),
        check_vma=False,
    )
```

profile of v0, /device:TPU:1, one launch (start us, length us, event | category | flops | bytes accessed | tf_op | source)
XLA Modules:
  0.0 353.1 jit_solution(14736364626011634218)
XLA Ops:
  8.4 59.7 %all-gather.12.cloned.1.call-done = bf16[1024,3072]{1,0:T(8,128)(2,1)} async-done(((bf16[32,3072]{1,0:T(8,128)(2,1)}), bf16[1024,3072]{1,0:T(8,128)(2,1)}) %all-gather.12.cloned.1.call-update) | async-done | bytes 6291472 | tf_op jit(solution)/shard_map/all_gather | solution.py:19
  68.1 4.1 %fusion.20 = bf16[1024,512]{1,0:T(8,128)(2,1)} fusion(bf16[512,1024]{1,0:T(8,128)(2,1)} %bitcast.97, bf16[1024,3072]{1,0:T(8,128)(2,1)} %all-gather.12.cloned.1.call-done), kind=kOutput, calls=%fused_computation.26 | convolution fusion | flops 1074266112 | bytes 4194304 | tf_op jit(solution)/shard_map/dot_general | solution.py:62
  73.6 4.2 %fusion.23 = bf16[1024,512]{1,0:T(8,128)(2,1)} fusion(bf16[512,1024]{1,0:T(8,128)(2,1)} %bitcast.98, bf16[1024,3072]{1,0:T(8,128)(2,1)} %all-gather.12.cloned.1.call-done), kind=kOutput, calls=%fused_computation.27 | convolution fusion | flops 1074266112 | bytes 4194304 | tf_op jit(solution)/shard_map/dot_general | solution.py:62
  82.7 15.2 %all-gather.16.cloned.1.call-done = f32[4,8,128,128]{3,2,1,0:T(8,128)} async-done(((f32[2,8,128,128]{3,2,1,0:T(8,128)}), f32[4,8,128,128]{3,2,1,0:T(8,128)}) %all-gather.16.cloned.1.call-update) | async-done | bytes 2097168 | tf_op jit(solution)/shard_map/all_gather | solution.py:31
  100.6 51.2 %all-gather.22.cloned.1.call-done = f32[8,8,128,128]{3,2,1,0:T(8,128)} async-done(((f32[2,8,128,128]{3,2,1,0:T(8,128)}), f32[8,8,128,128]{3,2,1,0:T(8,128)}) %all-gather.22.cloned.1.call-update) | async-done | bytes 4194320 | tf_op jit(solution)/shard_map/all_gather | solution.py:31
  151.8 3.5 fusion.29
  155.3 4.0 %convert_bitcast_fusion.2 = bf16[128,8,8,128]{3,1,2,0:T(8,128)(2,1)S(1)} fusion(bf16[1024,1024]{1,0:T(8,128)(2,1)S(1)} %bitcast.79, bf16[1024,3072]{1,0:T(8,128)(2,1)} %all-gather.12.cloned.1.call-done), kind=kOutput, calls=%fused_computation.19 | convolution fusion | flops 2148532224 | bytes 6291456 | tf_op jit(solution)/shard_map/dot_general | solution.py:62
  161.2 4.1 %copy.36 = bf16[8,128,8,128]{3,1,2,0:T(8,128)(2,1)} copy(bf16[8,128,8,128]{1,0,3,2:T(8,128)(2,1)} %bitcast.82) | data formatting | bytes 4194304 | tf_op jit(solution)/shard_map/reshape | solution.py:111
  165.4 6.9 %all-to-all-start = ((bf16[8,128,8,128]{3,1,2,0:T(8,128)(2,1)}), bf16[8,128,8,128]{3,1,2,0:T(8,128)(2,1)}, u32[]{:S(2)}, u32[]{:S(2)}) async-start(bf16[8,128,8,128]{3,1,2,0:T(8,128)(2,1)} %copy.36), calls=%async_computation | async-start | bytes 4194304 | tf_op jit(solution)/shard_map/all_to_all | solution.py:114
  173.7 4.9 %fusion = f32[8,128,8,128]{3,1,0,2:T(8,128)} fusion(bf16[512,8,128,1]{0,2,1,3:T(8,128)(2,1)} %bitcast.92, bf16[512,8,128]{2,0,1:T(8,128)(2,1)} %copy.34, bf16[8,512]{1,0:T(8,128)(2,1)S(1)} %and_convert_fusion), kind=kOutput, calls=%fused_computation | convolution fusion | flops 1090519040 | bytes 6299648 | tf_op jit(solution)/shard_map/erhd,rhf->ehdf/dot_general | solution.py:100
  178.6 28.0 %all-gather.14.cloned.1.call-done = f32[4,2,8,128,128]{4,3,2,1,0:T(8,128)} async-done(((f32[1,2,8,128,128]{4,3,2,1,0:T(8,128)}), f32[4,2,8,128,128]{4,3,2,1,0:T(8,128)}) %all-gather.14.cloned.1.call-update) | async-done | bytes 4194320 | tf_op jit(solution)/shard_map/all_gather | solution.py:31
  206.6 5.2 %fusion.28 = f32[2,8,128,128]{3,2,1,0:T(8,128)S(1)} fusion(f32[4,2,8,128,128]{4,3,2,1,0:T(8,128)} %all-gather.14.cloned.1.call-done, f32[8,8,128,128]{3,2,1,0:T(8,128)} %all-gather.22.cloned.1.call-done, f32[4,8,128,128]{3,2,1,0:T(8,128)} %all-gather.16.cloned.1.call-done, pred[]{:T(512)S(6)} %gt.35, pred[]{:T(512)S(6)} %gt.36, pred[]{:T(512)S(6)} %gt.37, ...), kind=kLoop, calls=%fused_computation.31 | loop fusion | flops 4980736 | bytes 11534346 | tf_op jit(solution)/shard_map/mul | solution.py:109
  214.8 5.3 %copy.35 = f32[8,8,128,128]{2,3,1,0:T(8,128)} copy(f32[8,8,128,128]{3,2,1,0:T(8,128)} %multiply_reduce_fusion) | data formatting | bytes 8388608 | tf_op jit(solution)/shard_map/reduce_sum | solution.py:109
  220.1 3.9 %all-to-all-done = bf16[8,128,8,128]{3,1,2,0:T(8,128)(2,1)} async-done(((bf16[8,128,8,128]{3,1,2,0:T(8,128)(2,1)}), bf16[8,128,8,128]{3,1,2,0:T(8,128)(2,1)}, u32[]{:S(2)}, u32[]{:S(2)}) %all-to-all-start) | async-done | bytes 2097184 | tf_op jit(solution)/shard_map/all_to_all | solution.py:114
  224.0 10.6 %fusion.5 = f32[8,128,8,128]{1,3,2,0:T(8,128)} fusion(bf16[8,128,8,128]{3,1,2,0:T(8,128)(2,1)} %all-to-all-done, f32[8,8,128,128]{2,3,1,0:T(8,128)} %copy.35, f32[8,128,8,128]{3,1,0,2:T(8,128)} %fusion), kind=kOutput, calls=%fused_computation.12 | convolution fusion | flops 1611661312 | bytes 14680064 | tf_op jit(solution)/shard_map/ebhd,ehdf->ebhf/dot_general | solution.py:115
  234.6 4.7 %all-to-all-start.1 = ((f32[8,128,8,128]{1,3,2,0:T(8,128)}), f32[8,128,8,128]{1,3,2,0:T(8,128)}, u32[]{:S(2)}, u32[]{:S(2)}) async-start(f32[8,128,8,128]{1,3,2,0:T(8,128)} %fusion.5), calls=%async_computation.1 | async-start | bytes 8388608 | tf_op jit(solution)/shard_map/all_to_all | solution.py:118
  239.4 10.4 %all-gather.1 = bf16[128,1024]{1,0:T(8,128)(2,1)} all-gather(bf16[32,1024]{1,0:T(8,128)(2,1)S(1)} %copy-done.3), channel_id=3, replica_groups=mesh['leaf'=8,'trunk_0'=4,'trunk_1'=4,'trunk_2'=2] {'trunk_1'}, dimensions={0}, use_global_device_ids=true | all-gather | bytes 327680 | tf_op jit(solution)/shard_map/all_gather | solution.py:50
  250.1 27.0 %all-gather.18.cloned.1.call-done = bf16[16,32,1024]{2,1,0:T(8,128)(2,1)} async-done(((bf16[4,32,1024]{2,1,0:T(8,128)(2,1)}), bf16[16,32,1024]{2,1,0:T(8,128)(2,1)}) %all-gather.18.cloned.1.call-update) | async-done | bytes 1048592 | tf_op jit(solution)/shard_map/all_gather | solution.py:50
  277.2 20.3 %all-gather.20.cloned.1.call-done = bf16[8,4,32,1024]{3,2,1,0:T(8,128)(2,1)} async-done(((bf16[4,4,32,1024]{3,2,1,0:T(8,128)(2,1)}), bf16[8,4,32,1024]{3,2,1,0:T(8,128)(2,1)}) %all-gather.20.cloned.1.call-update) | async-done | bytes 2097168 | tf_op jit(solution)/shard_map/all_gather | solution.py:50
  300.7 4.0 %convert_bitcast_fusion.1 = bf16[128,8,8,128]{3,1,2,0:T(8,128)(2,1)S(1)} fusion(bf16[1024,1024]{1,0:T(8,128)(2,1)S(1)} %bitcast.80, bf16[1024,3072]{1,0:T(8,128)(2,1)} %all-gather.12.cloned.1.call-done), kind=kOutput, calls=%fused_computation.18 | convolution fusion | flops 2148532224 | bytes 6291456 | tf_op jit(solution)/shard_map/dot_general | solution.py:62
  306.6 4.0 %convert_bitcast_fusion = bf16[128,8,8,128]{3,1,2,0:T(8,128)(2,1)S(1)} fusion(bf16[1024,1024]{1,0:T(8,128)(2,1)S(1)} %bitcast.81, bf16[1024,3072]{1,0:T(8,128)(2,1)} %all-gather.12.cloned.1.call-done), kind=kOutput, calls=%fused_computation.17 | convolution fusion | flops 2148532224 | bytes 6291456 | tf_op jit(solution)/shard_map/dot_general | solution.py:62
  312.6 18.8 %all-to-all-done.1 = f32[8,128,8,128]{1,3,2,0:T(8,128)} async-done(((f32[8,128,8,128]{1,3,2,0:T(8,128)}), f32[8,128,8,128]{1,3,2,0:T(8,128)}, u32[]{:S(2)}, u32[]{:S(2)}) %all-to-all-start.1) | async-done | bytes 4194336 | tf_op jit(solution)/shard_map/all_to_all | solution.py:118
  331.4 8.2 %multiply_reduce_fusion.1 = (f32[8,128,8]{1,2,0:T(8,128)S(1)}, f32[8,128,8,128]{1,3,2,0:T(8,128)}) fusion(f32[8,128,8,128]{1,3,2,0:T(8,128)} %all-to-all-done.1, bf16[8,128,8,128]{3,1,2,0:T(8,128)(2,1)} %copy.36, bf16[8,128,8,128]{1,0,3,2:T(8,128)(2,1)} %bitcast.84, pred[128,128]{1,0:T(8,128)(4,1)S(1)} %iota_compare_fusion, bf16[8,128,8,128]{1,0,3,2:T(8,128)(2,1)} %bitcast.83), kind=kOutput, calls=%fused_computation.8 | convolution fusion | flops 542105600 | bytes 14729216 | tf_op jit(solution)/shard_map/shbc,schf->sbhf/dot_general | solution.py:123
  342.6 3.7 %select_convert_fusion = bf16[8,128,1024]{2,1,0:T(8,128)(2,1)} fusion(pred[8,128]{1,0:T(8,128)(4,1)S(1)} %iota_compare_fusion.2, bf16[8,128,1024]{1,2,0:T(8,128)(2,1)S(1)} %bitcast.87, bf16[1024,1024,1]{1,0,2:T(8,128)(2,1)S(1)} %bitcast.88), kind=kOutput, calls=%fused_computation.6 | convolution fusion | flops 2149580800 | bytes 6292480 | tf_op jit(solution)/shard_map/dot_general | solution.py:62
  (44 shorter events, 27.5 us)
Async XLA Ops:
  6.5 148.8 %copy-start = (bf16[8,128,1024]{2,1,0:T(8,128)(2,1)S(1)}, bf16[8,128,1024]{2,1,0:T(8,128)(2,1)}, u32[]{:S(2)}) copy-start(bf16[8,128,1024]{2,1,0:T(8,128)(2,1)} %param.10) | copy-start | bytes 6291460
  6.5 61.5 %all-gather.12.cloned.1.call-start = ((), (), s32[]{:S(2)}) async-start(), calls=%async_computation.2 | async-start | bytes 6488064 | tf_op jit(solution)/shard_map/all_gather | solution.py:19
  8.3 89.6 %all-gather.16.cloned.1.call-start = ((), (), s32[]{:S(2)}) async-start(), calls=%async_computation.4 | async-start | bytes 3145728 | tf_op jit(solution)/shard_map/all_gather | solution.py:31
  82.6 69.2 %all-gather.22.cloned.1.call-start = ((), (), s32[]{:S(2)}) async-start(), calls=%async_computation.7 | async-start | bytes 5242880 | tf_op jit(solution)/shard_map/all_gather | solution.py:31
  100.5 106.1 %all-gather.14.cloned.1.call-start = ((), (), s32[]{:S(2)}) async-start(), calls=%async_computation.3 | async-start | bytes 5242880 | tf_op jit(solution)/shard_map/all_gather | solution.py:31
  165.4 6.9 %copy-start.4 = (s32[1,1,8]{2,1,0:T(1,128)S(1)}, s32[1,1,8]{2,1,0:T(1,128)}, u32[]{:S(2)}) copy-start(s32[1,1,8]{2,1,0:T(1,128)} %param.12) | copy-start | bytes 100
  165.4 7.0 %copy-start.5 = (s32[1,1,8]{2,1,0:T(1,128)S(1)}, s32[1,1,8]{2,1,0:T(1,128)}, u32[]{:S(2)}) copy-start(s32[1,1,8]{2,1,0:T(1,128)} %param.11) | copy-start | bytes 100
  165.4 7.0 %copy-start.1 = (bf16[1024,512]{1,0:T(8,128)(2,1)S(1)}, bf16[1024,512]{1,0:T(8,128)(2,1)}, u32[]{:S(2)}) copy-start(bf16[1024,512]{1,0:T(8,128)(2,1)} %fusion.20) | copy-start | bytes 3145732
  165.4 58.6 %all-to-all-start = ((bf16[8,128,8,128]{3,1,2,0:T(8,128)(2,1)}), bf16[8,128,8,128]{3,1,2,0:T(8,128)(2,1)}, u32[]{:S(2)}, u32[]{:S(2)}) async-start(bf16[8,128,8,128]{3,1,2,0:T(8,128)(2,1)} %copy.36), calls=%async_computation | async-start | bytes 4194304 | tf_op jit(solution)/shard_map/all_to_all | solution.py:114
  234.6 4.8 %copy-start.3 = (bf16[32,1024]{1,0:T(8,128)(2,1)S(1)}, bf16[32,1024]{1,0:T(8,128)(2,1)}, u32[]{:S(2)}) copy-start(bf16[32,1024]{1,0:T(8,128)(2,1)} %param.17) | copy-start | bytes 196612
  234.6 42.5 %copy-start.6 = (s32[8]{0:T(128)S(1)}, s32[8]{0:T(128)}, u32[]{:S(2)}) copy-start(s32[8]{0:T(128)} %param.13) | copy-start | bytes 100
  234.6 96.8 %all-to-all-start.1 = ((f32[8,128,8,128]{1,3,2,0:T(8,128)}), f32[8,128,8,128]{1,3,2,0:T(8,128)}, u32[]{:S(2)}, u32[]{:S(2)}) async-start(f32[8,128,8,128]{1,3,2,0:T(8,128)} %fusion.5), calls=%async_computation.1 | async-start | bytes 8388608 | tf_op jit(solution)/shard_map/all_to_all | solution.py:118
  239.3 37.8 %all-gather.18.cloned.1.call-start = ((), (), s32[]{:S(2)}) async-start(), calls=%async_computation.5 | async-start | bytes 1310720 | tf_op jit(solution)/shard_map/all_gather | solution.py:50
  249.8 47.7 %all-gather.20.cloned.1.call-start = ((), (), s32[]{:S(2)}) async-start(), calls=%async_computation.6 | async-start | bytes 3145728 | tf_op jit(solution)/shard_map/all_gather | solution.py:50
  339.6 3.0 copy-start.2
Sparse Core Ops, SparseCore 0:
  9.9 58.1 all-gather.11
  82.7 15.0 all-gather.15
  100.7 51.1 all-gather.21
  155.4 51.1 all-gather.13
  249.9 27.1 all-gather.17
  278.7 18.7 all-gather.19
where the time goes:
time: 357 us; the launch traced here: 353 us
  waiting for transfers between devices  224 us (63%)
  matrix products  50.4 us (14%)
  local copies, waits for them, and re-layouts  23.3 us (7%)
  other arithmetic  19.2 us (5%)
  between operations  13.6 us (4%)
  starting transfers between devices  12 us (3%)
  blocking collectives  10.4 us (3%)
    all_gather x3, waiting for transfers between devices, entering(): pieces = lax.all_gather(subtotal, axis)  94.4 us
    all_gather x1, waiting for transfers between devices, side_by_side(): lax.all_gather(both, axis, axis=dim, tiled=True)  59.7 us
    all_gather x2, waiting for transfers between devices, all_blocks(): parts = lax.all_gather(parts, axes[k])  47.3 us
    dot_general x6, matrix products, matmul(): return jnp.dot(left, right, preferred_element_type=jnp.float32)  24 us
    all_to_all x1, waiting for transfers between devices, shards(): lax.all_to_all(held_inter, 'leaf', split_axis=0, concat_axis=0, tiled=True)  18.8 us
    dot_general x1, matrix products, shards(): jnp.einsum('ebhd,ehdf->ebhf', arrived.astype(jnp.float32), fork_state, pr...  10.6 us
    all_gather x1, blocking collectives, all_blocks(): parts = lax.all_gather(parts, axes[k])  10.4 us
    dot_general x1, matrix products, shards(): jnp.einsum('shbc,schf->sbhf', weights, value, preferred_element_type=jnp....  8.24 us
  transfers between devices with their start and end apart: 8, of which 8 were waited for; matrix products, arithmetic and copies ran while one was open for 13% of the time, Pallas kernels for 0%

commit v1 on v0

v1 whole, which is shorter than its diff:
```python
import jax
import jax.numpy as jnp
from jax import lax
from jax.experimental import pallas as pl
from jax.experimental.pallas import tpu as pltpu
from jax.sharding import Mesh
from jax.sharding import PartitionSpec as P

AXES = ("leaf", "ty", "tx", "tc")
TRUNK = AXES[1:]
MESH = pl.DeviceIdType.MESH
BF = jnp.bfloat16
F32 = jnp.float32
H = 8
DH = 128
LEAF = 8
ROW = 4
AHEAD = 3


def dot(left, right):
    return jnp.dot(left, right, preferred_element_type=F32)


def kernel(
    trunk_hbm, branch_hbm, offset, which, wq_hbm, wk_hbm, wv_hbm, wo_hbm,
    normed_hbm, ofull_hbm,
    trunk, branch, kw, vw, qw, ow, key_t, val, tot, crecv, xsend, xrecv, ysend, yrecv,
    own, psend, precv, sbuf, sv, kb, qwb, normed,
    load_sem, kw_load, qo_load, w1s, w1r, w2s, w2r, w3s, w3r, u1s, u1r, u2s, u2r, u3s, u3r,
    cs, cr, xs, xr, ys, yr, ps, pr, zs, zr, out_sem,
):
    leaf = lax.axis_index("leaf")
    ty = lax.axis_index("ty")
    tx = lax.axis_index("tx")
    tc = lax.axis_index("tc")
    here = {"leaf": (leaf, LEAF), "ty": (ty, ROW), "tx": (tx, ROW), "tc": (tc, 2)}

    def peer(axis, k):
        index, size = here[axis]
        return {axis: lax.rem(index + k, size)}

    def remote(src, dst, send, recv, axis, k):
        return pltpu.make_async_remote_copy(
            src_ref=src, dst_ref=dst, send_sem=send, recv_sem=recv,
            device_id=peer(axis, k), device_id_type=MESH,
        )

    def lanes(h, width):
        return pl.ds(pl.multiple_of(h * width, width), width)

    load_trunk = pltpu.make_async_copy(trunk_hbm, trunk, load_sem.at[0])
    load_branch = pltpu.make_async_copy(branch_hbm, branch, load_sem.at[1])

    def load_kv(h):
        return (
            pltpu.make_async_copy(wk_hbm.at[:, lanes(h, DH)], kw.at[h, ty, tx, tc], kw_load.at[h, 0]),
            pltpu.make_async_copy(wv_hbm.at[:, lanes(h, DH)], vw.at[h, ty, tx, tc], kw_load.at[h, 1]),
        )

    def load_qo(p):
        return (
            pltpu.make_async_copy(wq_hbm.at[:, lanes(p, 256)], qw.at[p, ty, tx, tc], qo_load.at[p, 0]),
            pltpu.make_async_copy(wo_hbm.at[:, lanes(p, 256)], ow.at[p, ty, tx, tc], qo_load.at[p, 1]),
        )

    def ways(first, second, s1, r1, s2, r2, s3, r3):
        def one(g):
            out = []
            for k in range(1, ROW):
                a, b = first.at[g, ty, tx, tc], second.at[g, ty, tx, tc]
                out.append(remote(a, a, s1.at[g, k - 1], r1.at[g, k - 1], "tx", k))
                out.append(remote(b, b, s1.at[g, k + 2], r1.at[g, k + 2], "ty", k))
            return out

        def two(g):
            out = []
            for k in range(1, ROW):
                a, b = first.at[g, ty, :, tc], second.at[g, :, tx, tc]
                out.append(remote(a, a, s2.at[g, k - 1], r2.at[g, k - 1], "ty", k))
                out.append(remote(b, b, s2.at[g, k + 2], r2.at[g, k + 2], "tx", k))
            return out

        def three(g):
            a, b = first.at[g, :, :, tc], second.at[g, :, :, tc]
            return [
                remote(a, a, s3.at[g, 0], r3.at[g, 0], "tc", 1),
                remote(b, b, s3.at[g, 1], r3.at[g, 1], "tc", 1),
            ]

        return one, two, three

    kv1, kv2, kv3 = ways(kw, vw, w1s, w1r, w2s, w2r, w3s, w3r)
    qo1, qo2, qo3 = ways(qw, ow, u1s, u1r, u2s, u2r, u3s, u3r)

    def start(copies):
        for c in copies:
            c.start()

    def arrive(copies):
        for c in copies:
            c.wait_recv()

    def sent(copies):
        for c in copies:
            c.wait_send()

    def copy_tot(h):
        return [remote(tot.at[h, 1 - tc], crecv.at[h], cs.at[h], cr.at[h], "tc", 1)]

    def copy_x(h):
        return [
            remote(xsend.at[h], xrecv.at[h, k - 1], xs.at[h, k - 1], xr.at[h, k - 1], "tx", k)
            for k in range(1, ROW)
        ]

    def copy_y(h):
        return [
            remote(ysend.at[h], yrecv.at[h, k - 1], ys.at[h, k - 1], yr.at[h, k - 1], "ty", k)
            for k in range(1, ROW)
        ]

    def copy_p(h):
        return [remote(psend.at[h], precv.at[h], ps.at[h], pr.at[h], "tc", 1)]

    def copy_z(h, k):
        return remote(
            sbuf.at[h, k], sv.at[h, leaf, pl.ds(0, DH)], zs.at[h, k - 1], zr.at[h, k - 1], "leaf", k
        )

    @pl.loop(0, H)
    def _(h):
        start(load_kv(h))

    load_trunk.start()

    @pl.loop(0, 4)
    def _(p):
        start(load_qo(p))

    load_branch.start()

    barrier = pltpu.get_barrier_semaphore()
    partners = (
        [("leaf", k) for k in range(1, LEAF)]
        + [("ty", k) for k in range(1, ROW)]
        + [("tx", k) for k in range(1, ROW)]
        + [("tc", 1)]
    )
    for axis, k in partners:
        pl.semaphore_signal(barrier, inc=1, device_id=peer(axis, k), device_id_type=MESH)
    pl.semaphore_wait(barrier, len(partners))

    @pl.loop(0, H)
    def _(h):
        for c in load_kv(h):
            c.wait()
        start(kv1(h))

    @pl.loop(0, AHEAD)
    def _(h):
        arrive(kv1(h))
        start(kv2(h))

    arrive(kv2(0))
    start(kv3(0))
    load_trunk.wait()

    @pl.loop(0, 4)
    def _(p):
        for c in load_qo(p):
            c.wait()
        start(qo1(p))

    load_branch.wait()

    def weights(h):
        return jnp.concatenate([kw[h].reshape(1024, DH), vw[h].reshape(1024, DH)], axis=1)

    def flag(cond):
        return jnp.where(cond, 1.0, 0.0).astype(F32)

    def stage1(h):
        arrive(kv3(h))
        w = weights(h)
        for r in range(2):
            both = dot(trunk[r], w)
            value = both[:, DH:].astype(BF)
            turned = both[:, :DH].T.astype(BF)
            key_t[h, r] = turned
            val[h, r] = value
            tot[h, r] = dot(turned, value)
        start(copy_tot(h))

    def stage2(h):
        arrive(copy_tot(h))
        xsend[h] = (tot[h, tc] + crecv[h]).astype(BF)
        start(copy_x(h))

    def stage3(h):
        arrive(copy_x(h))
        row = tot[h, tc] + crecv[h]
        for k in range(ROW - 1):
            row = row + xrecv[h, k].astype(F32)
        ysend[h] = row.astype(BF)
        start(copy_y(h))

    def stage4(h):
        arrive(copy_y(h))
        before = jnp.zeros((DH, DH), F32)
        for k in range(1, ROW):
            before = before + flag(ty >= k) * yrecv[h, k - 1].astype(F32)
            before = before + flag(tx >= k) * xrecv[h, k - 1].astype(F32)
        own[h] = before + flag(tc == 1) * crecv[h]
        psend[h] = before + flag(tc == 0) * tot[h, tc]
        start(copy_p(h))

    def stage5(h):
        arrive(copy_p(h))
        position = lax.broadcasted_iota(jnp.int32, (DH, 256), 1)
        for k in (4, 3, 5, 2, 6, 1, 7, 0):
            lane = lax.rem(leaf + k, LEAF)
            tree = which[lane]
            kept = jnp.where(position < offset[lane], key_t[h, tree].astype(F32), 0.0).astype(BF)
            base = jnp.where(tree == tc, own[h], precv[h])
            state = (base + dot(kept, val[h, tree])).astype(BF)
            if k == 0:
                sv[h, leaf, pl.ds(0, DH), :] = state
            else:
                sbuf[h, k] = state
                copy_z(h, k).start()

    def branch_kv(h):
        @pl.loop(0, 4)
        def _(i):
            both = dot(branch[i], weights(h)).astype(BF)
            for j in range(2):
                part = both[j * DH : (j + 1) * DH]
                kb[h, 2 * i + j] = part[:, :DH]
                sv[h, 2 * i + j, pl.ds(DH, DH), :] = part[:, DH:]

    @pl.loop(0, H + 4)
    def _(j):
        @pl.when(j >= 4)
        def _():
            stage5(j - 4)

        @pl.when((j >= 3) & (j < H + 3))
        def _():
            stage4(j - 3)

        @pl.when((j >= 2) & (j < H + 2))
        def _():
            stage3(j - 2)

        @pl.when((j >= 1) & (j < H + 1))
        def _():
            stage2(j - 1)

        @pl.when(j < H)
        def _():
            stage1(j)

        @pl.when(j + AHEAD < H)
        def _():
            arrive(kv1(j + AHEAD))
            start(kv2(j + AHEAD))

        @pl.when(j + 1 < H)
        def _():
            arrive(kv2(j + 1))
            start(kv3(j + 1))

        @pl.when((j >= 4) & (j < 8))
        def _():
            arrive(qo1(j - 4))
            start(qo2(j - 4))

        @pl.when((j >= 6) & (j < 10))
        def _():
            arrive(qo2(j - 6))
            start(qo3(j - 6))

        @pl.when(j < H)
        def _():
            branch_kv(j)

    rows = lax.broadcasted_iota(jnp.int32, (DH, DH), 0)
    columns = lax.broadcasted_iota(jnp.int32, (DH, DH), 1)

    @pl.loop(0, 4)
    def _(p):
        arrive(qo3(p))
        out = pltpu.make_async_copy(ow.at[p], ofull_hbm.at[:, :, :, :, lanes(p, 256)], out_sem.at[p])
        out.start()

        @pl.loop(0, 4)
        def _(i):
            both = dot(branch[i], qw[p].reshape(1024, 256)).astype(BF)
            for j in range(2):
                for u in range(2):
                    qwb[2 * p + u, 2 * i + j, :, pl.ds(0, DH)] = both[
                        j * DH : (j + 1) * DH, u * DH : (u + 1) * DH
                    ]
            for j in range(2):
                for u in range(2):
                    query = both[j * DH : (j + 1) * DH, u * DH : (u + 1) * DH]
                    scores = lax.dot_general(
                        query, kb[2 * p + u, 2 * i + j], (((1,), (1,)), ((), ())), preferred_element_type=F32
                    )
                    qwb[2 * p + u, 2 * i + j, :, pl.ds(DH, DH)] = jnp.where(
                        columns <= rows, scores, 0.0
                    ).astype(BF)

    @pl.loop(0, H)
    def _(h):
        for k in range(1, LEAF):
            copy_z(h, k).wait_recv()

        @pl.loop(0, LEAF)
        def _(s):
            numerator = dot(qwb[h, s], sv[h, s])
            meansq = jnp.mean(numerator * numerator, axis=-1, keepdims=True)
            normed[s, :, lanes(h, DH)] = (numerator * lax.rsqrt(meansq + 1e-06)).astype(BF)

        out = pltpu.make_async_copy(
            normed.at[:, :, lanes(h, DH)], normed_hbm.at[:, :, lanes(h, DH)], out_sem.at[4 + h]
        )
        out.start()

    @pl.loop(0, H)
    def _(h):
        sent(kv1(h) + kv2(h) + kv3(h) + copy_tot(h) + copy_x(h) + copy_y(h) + copy_p(h))
        sent([copy_z(h, k) for k in range(1, LEAF)])
        pltpu.make_async_copy(
            normed.at[:, :, lanes(h, DH)], normed_hbm.at[:, :, lanes(h, DH)], out_sem.at[4 + h]
        ).wait()

    @pl.loop(0, 4)
    def _(p):
        sent(qo1(p) + qo2(p) + qo3(p))
        pltpu.make_async_copy(
            ow.at[p], ofull_hbm.at[:, :, :, :, lanes(p, 256)], out_sem.at[p]
        ).wait()


def shards(
    trunk_tokens, branch_tokens, fork_offset, fork_tree, branch_len, w_query, w_key, w_value, w_out
):
    slots, blen, width = branch_tokens.shape
    dma = pltpu.SemaphoreType.DMA
    anywhere = pl.BlockSpec(memory_space=pl.ANY)
    small = pl.BlockSpec(memory_space=pltpu.SMEM)
    square = (DH, DH)
    vm = pltpu.VMEM
    normed, ofull = pl.pallas_call(
        kernel,
        out_shape=(
            jax.ShapeDtypeStruct((slots, blen, H * DH), BF),
            jax.ShapeDtypeStruct((ROW, ROW, 2, 32, width), BF),
        ),
        in_specs=[anywhere, anywhere, small, small] + [anywhere] * 4,
        out_specs=(anywhere, anywhere),
        scratch_shapes=[
            vm((2, 256, 1024), BF),
            vm((4, 256, 1024), BF),
            vm((H, ROW, ROW, 2, 32, DH), BF),
            vm((H, ROW, ROW, 2, 32, DH), BF),
            vm((4, ROW, ROW, 2, 32, 256), BF),
            vm((4, ROW, ROW, 2, 32, 256), BF),
            vm((H, 2, DH, 256), BF),
            vm((H, 2, 256, DH), BF),
            vm((H, 2) + square, F32),
            vm((H,) + square, F32),
            vm((H,) + square, BF),
            vm((H, ROW - 1) + square, BF),
            vm((H,) + square, BF),
            vm((H, ROW - 1) + square, BF),
            vm((H,) + square, F32),
            vm((H,) + square, F32),
            vm((H,) + square, F32),
            vm((H, LEAF) + square, BF),
            vm((H, LEAF, 256, DH), BF),
            vm((H, LEAF) + square, BF),
            vm((H, LEAF, DH, 256), BF),
            vm((LEAF, DH, H * DH), BF),
            dma((2,)), dma((H, 2)), dma((4, 2)),
            dma((H, 6)), dma((H, 6)), dma((H, 6)), dma((H, 6)), dma((H, 2)), dma((H, 2)),
            dma((4, 6)), dma((4, 6)), dma((4, 6)), dma((4, 6)), dma((4, 2)), dma((4, 2)),
            dma((H,)), dma((H,)), dma((H, 3)), dma((H, 3)), dma((H, 3)), dma((H, 3)), dma((H,)), dma((H,)),
            dma((H, 7)), dma((H, 7)), dma((12,)),
        ],
        compiler_params=pltpu.CompilerParams(
            collective_id=0, has_side_effects=True, vmem_limit_bytes=56 << 20
        ),
    )(
        trunk_tokens, branch_tokens.reshape(4, 256, width), fork_offset.reshape(-1), fork_tree.reshape(-1),
        w_query, w_key, w_value, w_out,
    )
    projected = jnp.dot(
        normed.reshape(slots * blen, H * DH), ofull.reshape(H * DH, width), preferred_element_type=F32
    )
    rows = jnp.arange(blen, dtype=jnp.int32)
    live = rows[None, :] < branch_len[:, None]
    projected = projected.reshape(slots, blen, width)
    return jnp.where(live[:, :, None], projected, 0.0).astype(BF)


def solution(mesh):
    split = Mesh(mesh.devices.reshape(LEAF, ROW, ROW, 2), AXES)
    return jax.shard_map(
        shards,
        mesh=split,
        in_specs=(
            P("leaf", TRUNK, None),
            P(AXES, None, None),
            P("leaf", TRUNK, None),
            P("leaf", TRUNK, None),
            P(AXES),
            P(TRUNK, None),
            P(TRUNK, None),
            P(TRUNK, None),
            P(TRUNK, None),
        ),
        out_specs=P(AXES, None, None),
        check_vma=False,
    )
```

time: 357 us -> 103 us (0.29); the launches traced: 353 us -> 103 us
  waiting for transfers between devices: 224 us -> 0 us
  Pallas kernels: 0 us -> 96.1 us
  matrix products: 50.4 us -> 5.87 us
  local copies, waits for them, and re-layouts: 23.3 us -> 0 us
  other arithmetic: 19.2 us -> 0.73 us
  between operations: 13.6 us -> 0.01 us
  starting transfers between devices: 12 us -> 0 us
  blocking collectives: 10.4 us -> 0 us
    all_gather x6 -> x0, waiting for transfers between devices: 201 us -> none  [the longest x3 94.4 us: entering(): pieces = lax.all_gather(subtotal, axis)]
    pallas_call x0 -> x1, Pallas kernels: none -> 96.1 us  [shards(): pl.pallas_call(kernel, out_shape=(jax.ShapeDtypeStruct((slots, blen, H *...]
    dot_general x10 -> x1, matrix products: 50.4 us -> 5.87 us  [shards(): jnp.dot(normed.reshape(slots * blen, H * DH), ofull.reshape(H * DH, width...]
    all_to_all x2 -> x0, waiting for transfers between devices: 22.7 us -> none  [the longest x1 18.8 us: shards(): lax.all_to_all(held_inter, 'leaf', split_axis=0, concat_axis=0, tiled=True)]
    all_to_all x2 -> x0, starting transfers between devices: 11.6 us -> none  [the longest x1 6.87 us: shards(): lax.all_to_all(query, 'leaf', split_axis=0, concat_axis=0, tiled=True)]
    all_gather x1 -> x0, blocking collectives: 10.4 us -> none  [all_blocks(): parts = lax.all_gather(parts, axes[k])]
    reshape x3 -> x0, local copies, waits for them, and re-layouts: 7.6 us -> none  [the longest x1 4.13 us: shards(): query = branch_query.astype(jnp.bfloat16).reshape(slots, blen, H, DH)]
    add x2 -> x0, other arithmetic: 6.1 us -> none  [add_states(): return earlier + later]
  transfers between devices with their start and end apart: 8 -> 0, of which waited for: 8 -> 0; matrix products, arithmetic and copies ran while one was open for 13% -> 0% of each run, Pallas kernels for 0% -> 0%
where the time goes in v1:
time: 103 us
  Pallas kernels  96.1 us (93%)
  matrix products  5.87 us (6%)
    pallas_call x1, Pallas kernels, shards(): pl.pallas_call(kernel, out_shape=(jax.ShapeDtypeStruct((slots, blen, H *...  96.1 us
    dot_general x1, matrix products, shards(): jnp.dot(normed.reshape(slots * blen, H * DH), ofull.reshape(H * DH, width...  5.87 us

profile of v1, /device:TPU:1, one launch (start us, length us, event | category | flops | bytes accessed | tf_op | source)
XLA Modules:
  0.0 102.7 jit_solution(12119327610315907929)
XLA Ops:
  0.0 0.7 iota_compare_fusion
  0.7 96.1 %shard_map.91 = (bf16[8,128,1024]{2,1,0:T(8,128)(2,1)}, bf16[4,4,2,32,1024]{4,3,2,1,0:T(8,128)(2,1)}) custom-call(bf16[2,256,1024]{2,1,0:T(8,128)(2,1)} %trunk_hbm.1, bf16[4,256,1024]{2,1,0:T(8,128)(2,1)} %bitcast.8, s32[8]{0:T(128)} %bitcast.9, s32[8]{0:T(128)} %bitcast.10, bf16[32,1024]{1,0:T(8,128)(2,1)} %wq_hbm.1, bf16[32,1024]{1,0:T(8,128)(2,1)} %wk_hbm.1, ...), custom_call_target="tpu_custom_call" | custom-call | tf_op jit(solution)/shard_map/pallas_call | solution.py:356
  96.9 5.9 %select_convert_fusion = bf16[8,128,1024]{2,1,0:T(8,128)(2,1)} fusion(pred[8,128]{1,0:T(8,128)(4,1)S(1)} %iota_compare_fusion, bf16[8,128,1024]{2,1,0:T(8,128)(2,1)} %get-tuple-element.7, bf16[1024,1024,1]{1,0,2:T(8,128)(2,1)} %bitcast.11), kind=kOutput, calls=%fused_computation | convolution fusion | flops 2149580800 | bytes 6292480 | tf_op jit(solution)/shard_map/dot_general | solution.py:400

commit v2 on v1

v2 whole, which is shorter than its diff:
```python
import jax
import jax.numpy as jnp
from jax import lax
from jax.experimental import pallas as pl
from jax.experimental.pallas import tpu as pltpu
from jax.sharding import Mesh
from jax.sharding import PartitionSpec as P

AXES = ("leaf", "ty", "tx", "tc")
TRUNK = AXES[1:]
MESH = pl.DeviceIdType.MESH
BF = jnp.bfloat16
F32 = jnp.float32
H = 8
DH = 128
LEAF = 8
ROW = 4


def dot(left, right):
    return jnp.dot(left, right, preferred_element_type=F32)


def kernel(
    trunk_hbm, branch_hbm, offset, which, length, wq_hbm, wk_hbm, wv_hbm, wo_hbm,
    result,
    trunk, branch, kw, vw, qw, ow, key_t, val, tot, crecv, xsend, xrecv, ysend, yrecv,
    carried, psend, sbuf, sv, kb, qwb, normed, acc,
    load_sem, w1r, w2r, w3r, u1r, u2r, u3r, cr, xr, yr, pr, zr, send, near,
):
    leaf = lax.axis_index("leaf")
    ty = lax.axis_index("ty")
    tx = lax.axis_index("tx")
    tc = lax.axis_index("tc")
    here = {"leaf": (leaf, LEAF), "ty": (ty, ROW), "tx": (tx, ROW), "tc": (tc, 2)}

    def peer(axis, k):
        index, size = here[axis]
        return {axis: lax.rem(index + k, size)}

    def remote(src, dst, send, recv, axis, k):
        return pltpu.make_async_remote_copy(
            src_ref=src, dst_ref=dst, send_sem=send, recv_sem=recv,
            device_id=peer(axis, k), device_id_type=MESH,
        )

    def lanes(h, width):
        return pl.ds(pl.multiple_of(h * width, width), width)

    def landed(view, sem):
        pltpu.make_async_copy(view, view, sem).wait()

    load_trunk = pltpu.make_async_copy(trunk_hbm, trunk, load_sem.at[0])
    load_branch = pltpu.make_async_copy(branch_hbm, branch, load_sem.at[1])

    def load_kv(h):
        pltpu.make_async_copy(wk_hbm.at[:, lanes(h, DH)], kw.at[h, ty, tx, tc], load_sem.at[2]).start()
        pltpu.make_async_copy(wv_hbm.at[:, lanes(h, DH)], vw.at[h, ty, tx, tc], load_sem.at[2]).start()

    def load_qo(p):
        pltpu.make_async_copy(wq_hbm.at[:, lanes(p, 256)], qw.at[p, ty, tx, tc], load_sem.at[3]).start()
        pltpu.make_async_copy(wo_hbm.at[:, lanes(p, 256)], ow.at[p, ty, tx, tc], load_sem.at[3]).start()

    def ways(first, second, s, r1, r2, r3):
        def one(g):
            for k in (2, 1, 3):
                a, b = first.at[g, ty, tx, tc], second.at[g, ty, tx, tc]
                remote(a, a, send.at[s], r1.at[g], "tx", k).start()
                remote(b, b, send.at[s], r1.at[g], "ty", k).start()

        def two(g):
            landed(first.at[0, 0, pl.ds(0, 3)], r1.at[g])
            for k in (2, 1, 3):
                a, b = first.at[g, ty, :, tc], second.at[g, :, tx, tc]
                remote(a, a, send.at[s + 1], r2.at[g], "ty", k).start()
                remote(b, b, send.at[s + 1], r2.at[g], "tx", k).start()

        def three(g):
            landed(first.at[0, pl.ds(0, 3)], r2.at[g])
            a, b = first.at[g, :, :, tc], second.at[g, :, :, tc]
            remote(a, a, send.at[s + 2], r3.at[g], "tc", 1).start()
            remote(b, b, send.at[s + 2], r3.at[g], "tc", 1).start()

        def ready(g):
            landed(first.at[0], r3.at[g])

        return one, two, three, ready

    kv_first, kv_second, kv_third, kv_ready = ways(kw, vw, 0, w1r, w2r, w3r)
    qo_first, qo_second, qo_third, qo_ready = ways(qw, ow, 3, u1r, u2r, u3r)

    def send_tot(h):
        remote(tot.at[h, 1 - tc], crecv.at[h], send.at[6], cr.at[h], "tc", 1).start()

    def send_x(h):
        for k in (2, 1, 3):
            remote(xsend.at[h], xrecv.at[h, k - 1], send.at[7], xr.at[h], "tx", k).start()

    def send_y(h):
        for k in (2, 1, 3):
            remote(ysend.at[h], yrecv.at[h, k - 1], send.at[8], yr.at[h], "ty", k).start()

    def send_p(h):
        remote(psend.at[h], carried.at[h, 1], send.at[9], pr.at[h], "tc", 1).start()

    def send_z(h, k):
        remote(sbuf.at[h, k], sv.at[h, leaf, pl.ds(0, DH)], send.at[10], zr.at[h], "leaf", k).start()

    barrier = pltpu.get_barrier_semaphore()
    partners = [("tc", 1), ("leaf", 1), ("leaf", LEAF - 1)]
    partners += [(axis, k) for axis in ("tx", "ty") for k in range(1, ROW)]
    for axis, k in partners:
        pl.semaphore_signal(barrier, inc=1, device_id=peer(axis, k), device_id_type=MESH)

    def vouch(i):
        for k in (1, LEAF - 1):
            pl.semaphore_signal(near.at[i], inc=1, device_id=peer("leaf", k), device_id_type=MESH)

    @pl.loop(0, H)
    def _(h):
        load_kv(h)

    load_trunk.start()
    load_branch.start()

    @pl.loop(0, 4)
    def _(p):
        load_qo(p)

    pl.semaphore_wait(barrier, len(partners))
    landed(kw.at[0, pl.ds(0, 2)], load_sem.at[2])
    kv_first(0)
    vouch(0)

    @pl.loop(1, 4)
    def _(h):
        kv_first(h)

    kv_second(0)
    kv_third(0)

    @pl.loop(1, 4)
    def _(h):
        kv_second(h)

    @pl.loop(4, H)
    def _(h):
        kv_first(h)

    load_trunk.wait()
    load_branch.wait()
    landed(qw.at[0, 0], load_sem.at[3])
    pl.semaphore_wait(near.at[0], 2)
    vouch(1)

    def weights(h):
        return jnp.concatenate([kw[h].reshape(1024, DH), vw[h].reshape(1024, DH)], axis=1)

    def flag(cond):
        return jnp.where(cond, 1.0, 0.0).astype(F32)

    def stage1(h):
        kv_ready(h)
        both = dot(trunk[...], weights(h))
        for r in range(2):
            part = both[r * 256 : (r + 1) * 256]
            value = part[:, DH:].astype(BF)
            turned = part[:, :DH].T.astype(BF)
            key_t[h, r] = turned
            val[h, r] = value
            tot[h, r] = dot(turned, value)
        send_tot(h)

    def stage2(h):
        landed(crecv.at[h], cr.at[h])
        xsend[h] = (tot[h, tc] + crecv[h]).astype(BF)
        send_x(h)

    def stage3(h):
        landed(xrecv.at[h], xr.at[h])
        row = tot[h, tc] + crecv[h]
        for k in range(ROW - 1):
            row = row + xrecv[h, k].astype(F32)
        ysend[h] = row.astype(BF)
        send_y(h)

    def stage4(h):
        landed(yrecv.at[h], yr.at[h])
        before = jnp.zeros((DH, DH), F32)
        for k in range(1, ROW):
            before = before + flag(ty >= k) * yrecv[h, k - 1].astype(F32)
            before = before + flag(tx >= k) * xrecv[h, k - 1].astype(F32)
        psend[h] = before + flag(tc == 0) * tot[h, tc]
        send_p(h)
        carried[h, 0] = before + flag(tc == 1) * crecv[h]

    shifts = (4, 3, 5, 2, 6, 1, 7, 0)

    def stage5(h):
        landed(psend.at[h], pr.at[h])
        position = lax.broadcasted_iota(jnp.int32, (DH, 256), 1)
        for k in shifts:
            lane = lax.rem(leaf + k, LEAF)
            tree = which[lane]
            kept = jnp.where(position < offset[lane], key_t[h, tree].astype(F32), 0.0).astype(BF)
            base = jnp.where(tree == tc, carried[h, 0], carried[h, 1])
            state = (base + dot(kept, val[h, tree])).astype(BF)
            if k == 0:
                sv[h, leaf, pl.ds(0, DH), :] = state
            else:
                sbuf[h, k] = state
        for k in shifts[:-1]:
            send_z(h, k)

    def branch_kv(h):
        both = dot(branch[...], weights(h)).astype(BF)
        for s in range(LEAF):
            part = both[s * DH : (s + 1) * DH]
            kb[h, s] = part[:, :DH]
            sv[h, s, pl.ds(DH, DH), :] = part[:, DH:]

    rows = lax.broadcasted_iota(jnp.int32, (DH, DH), 0)
    columns = lax.broadcasted_iota(jnp.int32, (DH, DH), 1)

    def branch_q(p):
        qo_ready(p)
        both = dot(branch[...], qw[p].reshape(1024, 256)).astype(BF)
        for s in range(LEAF):
            for u in range(2):
                query = both[s * DH : (s + 1) * DH, u * DH : (u + 1) * DH]
                scores = lax.dot_general(
                    query, kb[2 * p + u, s], (((1,), (1,)), ((), ())), preferred_element_type=F32
                )
                qwb[2 * p + u, s, :, pl.ds(0, DH)] = query
                qwb[2 * p + u, s, :, pl.ds(DH, DH)] = jnp.where(columns <= rows, scores, 0.0).astype(BF)

    @pl.loop(0, H + 4)
    def _(j):
        @pl.when(j < H)
        def _():
            stage1(j)
            branch_kv(j)

        @pl.when(j + 1 < H)
        def _():
            kv_third(j + 1)

        @pl.when(j == 0)
        def _():
            pl.semaphore_wait(near.at[1], 2)
            vouch(2)

        @pl.when((j >= 2) & (j < H + 2))
        def _():
            stage4(j - 2)

        @pl.when((j >= 1) & (j < H + 1))
        def _():
            stage3(j - 1)

        @pl.when(j < H)
        def _():
            stage2(j)

        @pl.when(j == 1)
        def _():
            pl.semaphore_wait(near.at[2], 2)

        @pl.when(j >= 8)
        def _():
            branch_q(j - 8)

        @pl.when((j >= 2) & (j < H + 2))
        def _():
            stage5(j - 2)

        @pl.when((j >= 2) & (j < 4))
        def _():
            kv_second(2 * j)
            kv_second(2 * j + 1)

        @pl.when((j >= 3) & (j < 7))
        def _():
            qo_first(j - 3)

        @pl.when((j >= 5) & (j < 9))
        def _():
            qo_second(j - 5)

        @pl.when((j >= 7) & (j < 11))
        def _():
            qo_third(j - 7)

    def finish(p):
        for u in range(2):
            h = 2 * p + u
            landed(sbuf.at[h, pl.ds(0, LEAF - 1)], zr.at[h])
            for s in range(LEAF):
                numerator = dot(qwb[h, s], sv[h, s])
                meansq = jnp.mean(numerator * numerator, axis=-1, keepdims=True)
                normed[s * DH : (s + 1) * DH, u * DH : (u + 1) * DH] = (
                    numerator * lax.rsqrt(meansq + 1e-06)
                ).astype(BF)

    def product(p, c):
        return dot(normed[...], ow[c, p].reshape(256, 256))

    landed(kw.at[pl.ds(0, 3), pl.ds(0, 2)], send.at[0])
    landed(kw.at[pl.ds(0, 6)], send.at[1])
    landed(kw, send.at[2])
    landed(qw.at[0, pl.ds(0, 3)], send.at[3])
    landed(qw.at[pl.ds(0, 3)], send.at[4])
    landed(qw, send.at[5])
    landed(crecv, send.at[6])
    landed(xrecv, send.at[7])
    landed(yrecv, send.at[8])
    landed(psend, send.at[9])

    finish(0)
    for c in range(4):
        acc[c] = product(0, c)

    @pl.loop(1, 3)
    def _(p):
        finish(p)
        for c in range(4):
            acc[c] += product(p, c)

    finish(3)
    place = lax.broadcasted_iota(jnp.int32, (DH, 256), 0)
    for c in range(4):
        total = acc[c] + product(3, c)
        for s in range(LEAF):
            result[s, :, c * 256 : (c + 1) * 256] = jnp.where(
                place < length[s], total[s * DH : (s + 1) * DH], 0.0
            ).astype(BF)

    landed(sbuf.at[pl.ds(0, LEAF - 1)], send.at[10])


def shards(
    trunk_tokens, branch_tokens, fork_offset, fork_tree, branch_len, w_query, w_key, w_value, w_out
):
    slots, blen, width = branch_tokens.shape
    dma = pltpu.SemaphoreType.DMA
    anywhere = pl.BlockSpec(memory_space=pltpu.HBM)
    small = pl.BlockSpec(memory_space=pltpu.SMEM)
    square = (DH, DH)
    vm = pltpu.VMEM
    return pl.pallas_call(
        kernel,
        out_shape=pltpu.VMEM((slots, blen, width), BF),
        in_specs=[anywhere, anywhere, small, small, small] + [anywhere] * 4,
        out_specs=pl.BlockSpec(memory_space=pltpu.VMEM),
        scratch_shapes=[
            vm((512, 1024), BF),
            vm((1024, 1024), BF),
            vm((H, ROW, ROW, 2, 32, DH), BF),
            vm((H, ROW, ROW, 2, 32, DH), BF),
            vm((4, ROW, ROW, 2, 32, 256), BF),
            vm((4, ROW, ROW, 2, 32, 256), BF),
            vm((H, 2, DH, 256), BF),
            vm((H, 2, 256, DH), BF),
            vm((H, 2) + square, F32),
            vm((H,) + square, F32),
            vm((H,) + square, BF),
            vm((H, ROW - 1) + square, BF),
            vm((H,) + square, BF),
            vm((H, ROW - 1) + square, BF),
            vm((H, 2) + square, F32),
            vm((H,) + square, F32),
            vm((H, LEAF) + square, BF),
            vm((H, LEAF, 256, DH), BF),
            vm((H, LEAF) + square, BF),
            vm((H, LEAF, DH, 256), BF),
            vm((1024, 256), BF),
            vm((4, 1024, 256), F32),
            dma((4,)),
            dma((H,)), dma((H,)), dma((H,)), dma((4,)), dma((4,)), dma((4,)),
            dma((H,)), dma((H,)), dma((H,)), dma((H,)), dma((H,)),
            dma((11,)), pltpu.SemaphoreType.REGULAR((3,)),
        ],
        compiler_params=pltpu.CompilerParams(
            collective_id=0, has_side_effects=True, vmem_limit_bytes=60 << 20
        ),
    )(
        trunk_tokens.reshape(-1, width), branch_tokens.reshape(-1, width),
        fork_offset.reshape(-1), fork_tree.reshape(-1), branch_len,
        w_query, w_key, w_value, w_out,
    )


def solution(mesh):
    split = Mesh(mesh.devices.reshape(LEAF, ROW, ROW, 2), AXES)
    return jax.shard_map(
        shards,
        mesh=split,
        in_specs=(
            P("leaf", TRUNK, None),
            P(AXES, None, None),
            P("leaf", TRUNK, None),
            P("leaf", TRUNK, None),
            P(AXES),
            P(TRUNK, None),
            P(TRUNK, None),
            P(TRUNK, None),
            P(TRUNK, None),
        ),
        out_specs=P(AXES, None, None),
        check_vma=False,
    )
```

time: 103 us -> 80.5 us (0.78)
  Pallas kernels: 96.1 us -> 79.1 us
  matrix products: 5.87 us -> 0 us
  local copies, waits for them, and re-layouts: 0 us -> 1.32 us
    pallas_call x1, Pallas kernels: 96.1 us -> 79.1 us  [shards(): pl.pallas_call(kernel, out_shape=pltpu.VMEM((slots, blen, width), BF), in...]
    dot_general x1 -> x0, matrix products: 5.87 us -> none  [shards(): jnp.dot(normed.reshape(slots * blen, H * DH), ofull.reshape(H * DH, width...]
    unnamed x0 -> x1, local copies, waits for them, and re-layouts: none -> 1.32 us
where the time goes in v2:
time: 80.5 us; the launch traced here: 80.4 us
  Pallas kernels  79.1 us (98%)
  local copies, waits for them, and re-layouts  1.32 us (2%)
    pallas_call x1, Pallas kernels, shards(): pl.pallas_call(kernel, out_shape=pltpu.VMEM((slots, blen, width), BF), in...  79.1 us

profile of v2, /device:TPU:1, one launch (start us, length us, event | category | flops | bytes accessed | tf_op | source)
XLA Modules:
  0.0 80.4 jit_solution(7079186622380450418)
XLA Ops:
  0.0 79.1 %shard_map.91 = bf16[8,128,1024]{2,1,0:T(8,128)(2,1)S(1)} custom-call(bf16[512,1024]{1,0:T(8,128)(2,1)} %bitcast.5, bf16[1024,1024]{1,0:T(8,128)(2,1)} %bitcast.4, s32[8]{0:T(128)} %bitcast.6, s32[8]{0:T(128)} %bitcast.7, s32[8]{0:T(128)} %length.1, bf16[32,1024]{1,0:T(8,128)(2,1)} %wq_hbm.1, bf16[32,1024]{1,0:T(8,128)(2,1)} %wk_hbm.1, ...), custom_call_target="tpu_custom_call" | custom-call | tf_op jit(solution)/shard_map/pallas_call | solution.py:350
  79.1 1.3 %copy.11 = bf16[8,128,1024]{2,1,0:T(8,128)(2,1)} copy(bf16[8,128,1024]{2,1,0:T(8,128)(2,1)S(1)} %shard_map.91) | data formatting | bytes 4194304

commit v3 on v2

--- a/solution.py
+++ b/solution.py
@@ -150,8 +150,6 @@
     load_trunk.wait()
     load_branch.wait()
     landed(qw.at[0, 0], load_sem.at[3])
-    pl.semaphore_wait(near.at[0], 2)
-    vouch(1)
 
     def weights(h):
         return jnp.concatenate([kw[h].reshape(1024, DH), vw[h].reshape(1024, DH)], axis=1)
@@ -239,40 +237,44 @@
         @pl.when(j < H)
         def _():
             stage1(j)
-            branch_kv(j)
-
-        @pl.when(j + 1 < H)
-        def _():
-            kv_third(j + 1)
+
+        @pl.when((j >= 2) & (j < H + 2))
+        def _():
+            stage4(j - 2)
+
+        @pl.when((j >= 1) & (j < H + 1))
+        def _():
+            stage3(j - 1)
+
+        @pl.when(j < H)
+        def _():
+            stage2(j)
 
         @pl.when(j == 0)
+        def _():
+            pl.semaphore_wait(near.at[0], 2)
+            vouch(1)
+
+        @pl.when(j == 1)
         def _():
             pl.semaphore_wait(near.at[1], 2)
             vouch(2)
 
+        @pl.when(j == 2)
+        def _():
+            pl.semaphore_wait(near.at[2], 2)
+
+        @pl.when(j >= 8)
+        def _():
+            branch_q(j - 8)
+
         @pl.when((j >= 2) & (j < H + 2))
         def _():
-            stage4(j - 2)
-
-        @pl.when((j >= 1) & (j < H + 1))
-        def _():
-            stage3(j - 1)
-
-        @pl.when(j < H)
-        def _():
-            stage2(j)
-
-        @pl.when(j == 1)
-        def _():
-            pl.semaphore_wait(near.at[2], 2)
-
-        @pl.when(j >= 8)
-        def _():
-            branch_q(j - 8)
-
-        @pl.when((j >= 2) & (j < H + 2))
-        def _():
             stage5(j - 2)
+
+        @pl.when(j + 1 < H)
+        def _():
+            kv_third(j + 1)
 
         @pl.when((j >= 2) & (j < 4))
         def _():
@@ -290,6 +292,10 @@
         @pl.when((j >= 7) & (j < 11))
         def _():
             qo_third(j - 7)
+
+        @pl.when(j < H)
+        def _():
+            branch_kv(j)
 
     def finish(p):
         for u in range(2):

time: 80.5 us -> 80.2 us (level)
  no operation moved by 1% of the time
where the time goes in v3:
time: 80.2 us; the launch traced here: 80.1 us
  Pallas kernels  78.7 us (98%)
  local copies, waits for them, and re-layouts  1.32 us (2%)
    pallas_call x1, Pallas kernels, shards(): pl.pallas_call(kernel, out_shape=pltpu.VMEM((slots, blen, width), BF), in...  78.7 us

profile of v3, /device:TPU:1, one launch (start us, length us, event | category | flops | bytes accessed | tf_op | source)
XLA Modules:
  0.0 80.1 jit_solution(16394785275919903873)
XLA Ops:
  0.0 78.7 %shard_map.91 = bf16[8,128,1024]{2,1,0:T(8,128)(2,1)S(1)} custom-call(bf16[512,1024]{1,0:T(8,128)(2,1)} %bitcast.5, bf16[1024,1024]{1,0:T(8,128)(2,1)} %bitcast.4, s32[8]{0:T(128)} %bitcast.6, s32[8]{0:T(128)} %bitcast.7, s32[8]{0:T(128)} %length.1, bf16[32,1024]{1,0:T(8,128)(2,1)} %wq_hbm.1, bf16[32,1024]{1,0:T(8,128)(2,1)} %wk_hbm.1, ...), custom_call_target="tpu_custom_call" | custom-call | tf_op jit(solution)/shard_map/pallas_call | solution.py:356
  78.8 1.3 %copy.11 = bf16[8,128,1024]{2,1,0:T(8,128)(2,1)} copy(bf16[8,128,1024]{2,1,0:T(8,128)(2,1)S(1)} %shard_map.91) | data formatting | bytes 4194304

commit v4 on v3

--- a/solution.py
+++ b/solution.py
@@ -90,18 +90,18 @@
     qo_first, qo_second, qo_third, qo_ready = ways(qw, ow, 3, u1r, u2r, u3r)
 
     def send_tot(h):
-        remote(tot.at[h, 1 - tc], crecv.at[h], send.at[6], cr.at[h], "tc", 1).start()
+        remote(tot.at[h, 1 - tc], crecv.at[h], send.at[6], cr.at[lax.rem(h, 2)], "tc", 1).start()
 
     def send_x(h):
         for k in (2, 1, 3):
-            remote(xsend.at[h], xrecv.at[h, k - 1], send.at[7], xr.at[h], "tx", k).start()
+            remote(xsend.at[h], xrecv.at[h, k - 1], send.at[7], xr.at[lax.rem(h, 2)], "tx", k).start()
 
     def send_y(h):
         for k in (2, 1, 3):
-            remote(ysend.at[h], yrecv.at[h, k - 1], send.at[8], yr.at[h], "ty", k).start()
+            remote(ysend.at[h], yrecv.at[h, k - 1], send.at[8], yr.at[lax.rem(h, 2)], "ty", k).start()
 
     def send_p(h):
-        remote(psend.at[h], carried.at[h, 1], send.at[9], pr.at[h], "tc", 1).start()
+        remote(psend.at[h], carried.at[h, 1], send.at[9], pr.at[lax.rem(h, 2)], "tc", 1).start()
 
     def send_z(h, k):
         remote(sbuf.at[h, k], sv.at[h, leaf, pl.ds(0, DH)], send.at[10], zr.at[h], "leaf", k).start()
@@ -131,17 +131,15 @@
     landed(kw.at[0, pl.ds(0, 2)], load_sem.at[2])
     kv_first(0)
     vouch(0)
+    kv_second(0)
 
     @pl.loop(1, 4)
     def _(h):
         kv_first(h)
 
-    kv_second(0)
     kv_third(0)
-
-    @pl.loop(1, 4)
-    def _(h):
-        kv_second(h)
+    kv_second(1)
+    kv_second(2)
 
     @pl.loop(4, H)
     def _(h):
@@ -170,12 +168,12 @@
         send_tot(h)
 
     def stage2(h):
-        landed(crecv.at[h], cr.at[h])
+        landed(crecv.at[h], cr.at[lax.rem(h, 2)])
         xsend[h] = (tot[h, tc] + crecv[h]).astype(BF)
         send_x(h)
 
     def stage3(h):
-        landed(xrecv.at[h], xr.at[h])
+        landed(xrecv.at[h], xr.at[lax.rem(h, 2)])
         row = tot[h, tc] + crecv[h]
         for k in range(ROW - 1):
             row = row + xrecv[h, k].astype(F32)
@@ -183,7 +181,7 @@
         send_y(h)
 
     def stage4(h):
-        landed(yrecv.at[h], yr.at[h])
+        landed(yrecv.at[h], yr.at[lax.rem(h, 2)])
         before = jnp.zeros((DH, DH), F32)
         for k in range(1, ROW):
             before = before + flag(ty >= k) * yrecv[h, k - 1].astype(F32)
@@ -195,7 +193,7 @@
     shifts = (4, 3, 5, 2, 6, 1, 7, 0)
 
     def stage5(h):
-        landed(psend.at[h], pr.at[h])
+        landed(psend.at[h], pr.at[lax.rem(h, 2)])
         position = lax.broadcasted_iota(jnp.int32, (DH, 256), 1)
         for k in shifts:
             lane = lax.rem(leaf + k, LEAF)
@@ -275,6 +273,10 @@
         @pl.when(j + 1 < H)
         def _():
             kv_third(j + 1)
+
+        @pl.when(j == 1)
+        def _():
+            kv_second(3)
 
         @pl.when((j >= 2) & (j < 4))
         def _():
@@ -383,7 +385,7 @@
             vm((4, 1024, 256), F32),
             dma((4,)),
             dma((H,)), dma((H,)), dma((H,)), dma((4,)), dma((4,)), dma((4,)),
-            dma((H,)), dma((H,)), dma((H,)), dma((H,)), dma((H,)),
+            dma((2,)), dma((2,)), dma((2,)), dma((2,)), dma((H,)),
             dma((11,)), pltpu.SemaphoreType.REGULAR((3,)),
         ],
         compiler_params=pltpu.CompilerParams(

time: 80.2 us -> 80 us (level)
  no operation moved by 1% of the time
where the time goes in v4:
time: 80 us; the launch traced here: 79.9 us
  Pallas kernels  78.6 us (98%)
  local copies, waits for them, and re-layouts  1.32 us (2%)
    pallas_call x1, Pallas kernels, shards(): pl.pallas_call(kernel, out_shape=pltpu.VMEM((slots, blen, width), BF), in...  78.6 us

profile of v4, /device:TPU:1, one launch (start us, length us, event | category | flops | bytes accessed | tf_op | source)
XLA Modules:
  0.0 79.9 jit_solution(14106263836978429565)
XLA Ops:
  0.0 78.6 %shard_map.91 = bf16[8,128,1024]{2,1,0:T(8,128)(2,1)S(1)} custom-call(bf16[512,1024]{1,0:T(8,128)(2,1)} %bitcast.5, bf16[1024,1024]{1,0:T(8,128)(2,1)} %bitcast.4, s32[8]{0:T(128)} %bitcast.6, s32[8]{0:T(128)} %bitcast.7, s32[8]{0:T(128)} %length.1, bf16[32,1024]{1,0:T(8,128)(2,1)} %wq_hbm.1, bf16[32,1024]{1,0:T(8,128)(2,1)} %wk_hbm.1, ...), custom_call_target="tpu_custom_call" | custom-call | tf_op jit(solution)/shard_map/pallas_call | solution.py:358
  78.6 1.3 %copy.11 = bf16[8,128,1024]{2,1,0:T(8,128)(2,1)} copy(bf16[8,128,1024]{2,1,0:T(8,128)(2,1)S(1)} %shard_map.91) | data formatting | bytes 4194304

commit v5 on v4

--- a/solution.py
+++ b/solution.py
@@ -78,11 +78,11 @@
         def three(g):
             landed(first.at[0, pl.ds(0, 3)], r2.at[g])
             a, b = first.at[g, :, :, tc], second.at[g, :, :, tc]
-            remote(a, a, send.at[s + 2], r3.at[g], "tc", 1).start()
-            remote(b, b, send.at[s + 2], r3.at[g], "tc", 1).start()
+            remote(a, a, send.at[s + 2], r3.at[lax.rem(g, 2)], "tc", 1).start()
+            remote(b, b, send.at[s + 2], r3.at[lax.rem(g, 2)], "tc", 1).start()
 
         def ready(g):
-            landed(first.at[0], r3.at[g])
+            landed(first.at[0], r3.at[lax.rem(g, 2)])
 
         return one, two, three, ready
 
@@ -384,7 +384,7 @@
             vm((1024, 256), BF),
             vm((4, 1024, 256), F32),
             dma((4,)),
-            dma((H,)), dma((H,)), dma((H,)), dma((4,)), dma((4,)), dma((4,)),
+            dma((H,)), dma((H,)), dma((2,)), dma((4,)), dma((4,)), dma((2,)),
             dma((2,)), dma((2,)), dma((2,)), dma((2,)), dma((H,)),
             dma((11,)), pltpu.SemaphoreType.REGULAR((3,)),
         ],

time: 80 us -> 79.9 us (level)
  no operation moved by 1% of the time
where the time goes in v5:
time: 79.9 us; the launch traced here: 79.8 us
  Pallas kernels  78.5 us (98%)
  local copies, waits for them, and re-layouts  1.32 us (2%)
    pallas_call x1, Pallas kernels, shards(): pl.pallas_call(kernel, out_shape=pltpu.VMEM((slots, blen, width), BF), in...  78.5 us

profile of v5, /device:TPU:1, one launch (start us, length us, event | category | flops | bytes accessed | tf_op | source)
XLA Modules:
  0.0 79.8 jit_solution(13493568468771309074)
XLA Ops:
  0.0 78.5 %shard_map.91 = bf16[8,128,1024]{2,1,0:T(8,128)(2,1)S(1)} custom-call(bf16[512,1024]{1,0:T(8,128)(2,1)} %bitcast.5, bf16[1024,1024]{1,0:T(8,128)(2,1)} %bitcast.4, s32[8]{0:T(128)} %bitcast.6, s32[8]{0:T(128)} %bitcast.7, s32[8]{0:T(128)} %length.1, bf16[32,1024]{1,0:T(8,128)(2,1)} %wq_hbm.1, bf16[32,1024]{1,0:T(8,128)(2,1)} %wk_hbm.1, ...), custom_call_target="tpu_custom_call" | custom-call | tf_op jit(solution)/shard_map/pallas_call | solution.py:358
  78.5 1.3 %copy.11 = bf16[8,128,1024]{2,1,0:T(8,128)(2,1)} copy(bf16[8,128,1024]{2,1,0:T(8,128)(2,1)S(1)} %shard_map.91) | data formatting | bytes 4194304
